TPU v7x, 32 devices: a whole 2x2x4 slice. The times are simulated.
32 devices in a mesh: groups: 2 (over y), cells: 4 (over z), corners: 2 (over x), kern: 2 (over core).
Axes of the slice: x: 2, y: 2, z: 4, core: 2. Of those that a mesh axis runs over, the one named last changes fastest.
Arguments:
- theta: float32 [64, 128, 128], P(('groups', 'cells')), parts along dimension 0, may hold values from -8 to 8
- target: bfloat16 [16, 128, 128], P(('groups', 'cells')), parts along dimension 0, may hold values from 0 to 1
- kernels: float32 [2, 2, 24, 35, 35], P(None, 'corners', 'kern'), may hold values from -25.33743 to 25.33743
- dose: float32 [2], P('corners'), may hold values from 0.6 to 1
- inst_owner: int32 [128, 1], P(('groups', 'cells')), parts along dimension 0, may hold values from 0 to 3; in each aligned block of 16 rows (0 to 15, 16 to 31, ...) at most 8 rows name the same one
- inst_local: int32 [128], P(('groups', 'cells')), parts along dimension 0, may hold values from 0 to 7
- inst_shift: int32 [128], P(('groups', 'cells')), parts along dimension 0, may hold values from 0 to 127
Outputs:
- theta_out: float32 [64, 128, 128], P(('groups', 'cells'), ('corners', 'kern')), parts along dimension 0
There are 2 independent parts, one for each index of `groups`. A program takes and returns all parts, laid end to end along the dimension named above; an argument that names none is the same for every part. Nothing has to cross between parts.
Inputs may be any that keep to these rules, and one draw needn't show every extreme that they name: `inst_owner`: within the rows of one device (aligned blocks of 16 rows) no owner is named by more than 8 rows, and in some block one owner is named by exactly 8.
All inputs are finite; a program needn't handle non-finite values.
Results may differ from a plain program's by a relative error of at most 0.003.
Values may be sent and summed in bfloat16 or wider, within the bound.
No kernel may reach another device: no remote copies, remote signals or barrier semaphores. Data moves between devices by JAX's collectives and lax.ppermute only.
A program may use at most 64 MiB of HBM per device.

v0:
```python
import math
import jax
import jax.numpy as jnp
from jax import lax
from jax.sharding import PartitionSpec as P

ITERS = 2
LR = 0.25
EPS = 1e-06
STEEP = 3.0


def tables(cell_size, freq_count):
    freqs = jnp.arange(freq_count, dtype=jnp.int32) - freq_count // 2
    pixels = jnp.arange(cell_size, dtype=jnp.int32)
    phase = (freqs[:, None] * pixels[None, :] % cell_size).astype(jnp.float32) * (
        2.0 * math.pi / cell_size
    )
    fwd_real = jnp.cos(phase)
    fwd_imag = -jnp.sin(phase)
    inv_real = fwd_real.T / cell_size
    inv_imag = -fwd_imag.T / cell_size
    return (fwd_real, fwd_imag, inv_real, inv_imag)


def spectrum(field, tabs):
    fwd_real, fwd_imag = (tabs[0], tabs[1])
    hp = lax.Precision.HIGHEST
    left_real = jnp.einsum("fx,txy->tfy", fwd_real, field, precision=hp)
    left_imag = jnp.einsum("fx,txy->tfy", fwd_imag, field, precision=hp)
    spec_real = jnp.einsum("tfy,gy->tfg", left_real, fwd_real, precision=hp) - jnp.einsum(
        "tfy,gy->tfg", left_imag, fwd_imag, precision=hp
    )
    spec_imag = jnp.einsum("tfy,gy->tfg", left_real, fwd_imag, precision=hp) + jnp.einsum(
        "tfy,gy->tfg", left_imag, fwd_real, precision=hp
    )
    return (spec_real, spec_imag)


def intensity(field, kern_real, kern_imag, tabs):
    inv_real, inv_imag = (tabs[2], tabs[3])
    hp = lax.Precision.HIGHEST
    spec_real, spec_imag = spectrum(field, tabs)

    def add_kernel(running, pair):
        resp_real = pair[0] * spec_real - pair[1] * spec_imag
        resp_imag = pair[0] * spec_imag + pair[1] * spec_real
        half_real = jnp.einsum("tfg,yg->tfy", resp_real, inv_real, precision=hp) - jnp.einsum(
            "tfg,yg->tfy", resp_imag, inv_imag, precision=hp
        )
        half_imag = jnp.einsum("tfg,yg->tfy", resp_real, inv_imag, precision=hp) + jnp.einsum(
            "tfg,yg->tfy", resp_imag, inv_real, precision=hp
        )
        near_real = jnp.einsum("xf,tfy->txy", inv_real, half_real, precision=hp) - jnp.einsum(
            "xf,tfy->txy", inv_imag, half_imag, precision=hp
        )
        near_imag = jnp.einsum("xf,tfy->txy", inv_real, half_imag, precision=hp) + jnp.einsum(
            "xf,tfy->txy", inv_imag, half_real, precision=hp
        )
        return (running + near_real * near_real + near_imag * near_imag, None)

    start = jnp.zeros(field.shape, jnp.float32)
    result, unused = lax.scan(add_kernel, start, (kern_real, kern_imag))
    return result


def per_device(theta, target, kernels, dose, inst_owner, inst_local, inst_shift):
    hp = lax.Precision.HIGHEST
    n_owners = lax.axis_size("cells")
    members = lax.axis_size(("corners", "kern"))
    member = lax.axis_index(("corners", "kern"))
    cells_here = theta.shape[0]
    cell_size = theta.shape[1]
    inst_count = inst_local.shape[0]
    tile_count = target.shape[0]
    slot_count = inst_count // tile_count
    capacity = max(2, 2 * inst_count // n_owners)
    band_rows = cell_size // members
    tabs = tables(cell_size, kernels.shape[3])
    dose_now = dose[0]
    wanted = target.astype(jnp.float32)
    kern_real = kernels[0, 0]
    kern_imag = kernels[1, 0]
    owners = inst_owner[:, 0]
    inst_iota = jnp.arange(inst_count, dtype=jnp.int32)
    same_owner = (owners[None, :] == owners[:, None]) & (inst_iota[None, :] < inst_iota[:, None])
    rank_in = jnp.sum(same_owner.astype(jnp.int32), axis=1)
    slot_index = owners * capacity + rank_in
    slot_hit = slot_index[:, None] == jnp.arange(n_owners * capacity, dtype=jnp.int32)[None, :]
    used_slot = jnp.any(slot_hit, axis=0)
    asked_local = jnp.sum(jnp.where(slot_hit, inst_local[:, None], 0), axis=0)
    request = jnp.where(used_slot, asked_local, -1).reshape(n_owners, capacity)
    asked = lax.all_to_all(request, "cells", split_axis=0, concat_axis=0, tiled=True)
    picker = (
        asked.reshape(-1)[:, None] == jnp.arange(cells_here, dtype=jnp.int32)[None, :]
    ).astype(jnp.float32)
    picker_half = picker.astype(jnp.bfloat16)
    slot_weights = slot_hit.astype(jnp.float32)
    cell_params = lax.dynamic_slice_in_dim(theta, member * band_rows, band_rows, 1)
    rows_here = cell_params.shape[1]
    for iteration in range(ITERS):
        mask_vals = jax.nn.sigmoid(cell_params).astype(jnp.bfloat16)
        outgoing = jnp.dot(
            picker_half, mask_vals.reshape(cells_here, -1), preferred_element_type=jnp.float32
        )
        outgoing = outgoing.astype(jnp.bfloat16).reshape(n_owners, capacity, rows_here, cell_size)
        received = lax.all_to_all(outgoing, "cells", split_axis=0, concat_axis=0, tiled=True)
        placed = jnp.take(
            received.reshape(n_owners * capacity, rows_here, cell_size), slot_index, axis=0
        )
        transmit = 2.0 * placed.astype(jnp.float32) - 1.0
        rolled = jax.vmap(lambda plane, offset: jnp.roll(plane, offset, axis=1))(
            transmit, inst_shift
        )
        tile_part = (
            jnp.sum(rolled.reshape(tile_count, slot_count, rows_here, cell_size), axis=1)
            / slot_count
        )
        tile_field = lax.all_gather(tile_part, ("corners", "kern"), axis=1, tiled=True)
        partial_image, pullback = jax.vjp(
            lambda plane: intensity(plane, kern_real, kern_imag, tabs), tile_field
        )
        image = lax.psum(partial_image.astype(jnp.bfloat16), "kern").astype(jnp.float32)
        resist = jax.nn.sigmoid(STEEP * (dose_now * image - 1.0))
        pressure = 2.0 * (resist - wanted) * resist * (1.0 - resist) * STEEP * dose_now
        tile_grad = pullback(pressure)[0]
        grad_part = lax.psum_scatter(
            tile_grad.astype(jnp.bfloat16), ("corners", "kern"), scatter_dimension=1, tiled=True
        ).astype(jnp.float32)
        inst_grads = jnp.repeat(grad_part, slot_count, axis=0)
        unrolled = jax.vmap(lambda plane, offset: jnp.roll(plane, -offset, axis=1))(
            inst_grads, inst_shift
        )
        slot_grads = jnp.dot(slot_weights.T, unrolled.reshape(inst_count, -1), precision=hp)
        slot_grads = slot_grads.reshape(n_owners, capacity, rows_here, cell_size)
        returned = lax.all_to_all(slot_grads, "cells", split_axis=0, concat_axis=0, tiled=True)
        cell_sums = jnp.dot(picker.T, returned.reshape(n_owners * capacity, -1), precision=hp)
        cell_sums = cell_sums.reshape(cells_here, rows_here, cell_size)
        squash = jax.nn.sigmoid(cell_params)
        gradient = cell_sums * (2.0 / slot_count) * squash * (1.0 - squash)
        squares = jnp.sum(gradient * gradient, axis=(1, 2))
        squares = lax.psum(squares, ("corners", "kern"))
        cell_params = (
            cell_params
            - LR * gradient / jnp.sqrt(squares / (cell_size * cell_size) + EPS)[:, None, None]
        )
    return cell_params


def solution(mesh):
    in_specs = (
        P(("groups", "cells"), None, None),
        P(("groups", "cells"), None, None),
        P(None, "corners", "kern", None, None),
        P("corners"),
        P(("groups", "cells"), None),
        P(("groups", "cells")),
        P(("groups", "cells")),
    )
    out_specs = P(("groups", "cells"), ("corners", "kern"), None)
    return jax.shard_map(
        per_device, mesh=mesh, in_specs=in_specs, out_specs=out_specs, check_vma=False
    )
```

profile of v0, /device:TPU:0, one launch (start us, length us, event | category | flops | bytes accessed | tf_op | source)
XLA Modules:
  0.0 497.6 jit_solution(15146863222986831006)
XLA Ops:
  9.6 6.3 %all-to-all-start = ((s32[4,1,8]{2,1,0:T(1,128)}), s32[4,1,8]{2,1,0:T(1,128)S(1)}, u32[]{:S(2)}, u32[]{:S(2)}) async-start(s32[4,1,8]{2,1,0:T(1,128)} %bitcast.3), calls=%async_computation | async-start | bytes 4096 | tf_op jit(solution)/shard_map/all_to_all | solution.py:93
  18.4 3.1 all-to-all-done
  23.7 3.4 all-to-all-start.1
  28.0 6.2 %all-to-all-done.1 = bf16[4,8,32,128]{3,2,1,0:T(8,128)(2,1)S(1)} async-done(((bf16[4,8,32,128]{3,2,1,0:T(8,128)(2,1)}), bf16[4,8,32,128]{3,2,1,0:T(8,128)(2,1)S(1)}, u32[]{:S(2)}, u32[]{:S(2)}) %all-to-all-start.1) | async-done | bytes 262176 | tf_op jit(solution)/shard_map/all_to_all | solution.py:107
  36.2 3.0 gather_fusion.1
  40.9 5.4 %all_gather.6 = f32[2,128,128]{2,1,0:T(8,128)S(1)} all-gather(f32[2,32,128]{2,1,0:T(8,128)S(1)} %broadcast_multiply_fusion.1), channel_id=1, replica_groups=mesh['groups'=2,'cells'=4,'corners'=2,'kern'=2] {'corners','kern'}, dimensions={1}, use_global_device_ids=true | all-gather | bytes 163840 | tf_op jit(solution)/shard_map/all_gather | solution.py:119
  49.9 63.0 %while.92 = (s32[]{:T(128)}, f32[2,128,128]{1,2,0:T(8,128)S(1)}, f32[12,1,35,35]{3,2,1,0:T(8,128)S(1)}, f32[12,1,35,35]{3,2,1,0:T(8,128)S(1)}, f32[12,2,128,128]...) while((s32[]{:T(128)}, f32[2,128,128]{1,2,0:T(8,128)S(1)}, ...), condition=%wide.region_5.8_spmd.clone.clone.clone.clone, body=%wide.region_4.7_spmd.clone.clone.clone.clone.sunk | while | flops 70917336 | bytes 2136583 | solution.py:63
  114.6 16.4 %all-reduce.8.cloned.1.call-done = bf16[2,128,128]{1,2,0:T(8,128)(2,1)} async-done(((bf16[2,128,128]{1,2,0:T(8,128)(2,1)}), bf16[2,128,128]{1,2,0:T(8,128)(2,1)}) %all-reduce.8.cloned.1.call-update) | async-done | bytes 65552 | tf_op jit(solution)/shard_map/psum | solution.py:123
  132.0 56.9 %while.93 = (s32[]{:T(128)}, f32[2,35,35]{2,1,0:T(8,128)S(1)}, f32[2,35,35]{2,1,0:T(8,128)S(1)}, f32[12,1,35,35]{3,2,1,0:T(8,128)S(1)}, f32[12,2,128,128]{2,3,1,...) while((s32[]{:T(128)}, f32[2,35,35]{2,1,0:T(8,128)S(1)}, ...), condition=%wide.region_8.11_spmd.clone.clone.clone.clone, body=%wide.region_7.10_spmd.clone.clone.clone.clone.sunk | while | flops 70994280 | bytes 1536399 | solution.py:63
  193.2 31.6 %all-reduce.12.cloned.1.call-done = bf16[2,128,128]{2,0,1:T(2,128)(2,1)} async-done(((bf16[2,128,128]{2,0,1:T(2,128)(2,1)}), bf16[2,128,128]{2,0,1:T(2,128)(2,1)}) %all-reduce.12.cloned.1.call-update) | async-done | bytes 65552
  226.8 3.0 gather_fusion.2
  232.0 17.8 %all_to_all.26 = f32[4,8,32,128]{3,1,2,0:T(8,128)S(1)} all-to-all(f32[4,8,32,128]{3,1,2,0:T(8,128)S(1)} %fusion.356), channel_id=1, replica_groups=mesh['groups'=2,'cells'=4,'corners'=2,'kern'=2] {'cells'}, dimensions={0} | all-to-all | bytes 1048576 | tf_op jit(solution)/shard_map/all_to_all | solution.py:136
  250.2 5.7 %psum.29 = f32[8]{0:T(128)S(1)} all-reduce(f32[8]{0:T(128)S(1)} %get-tuple-element.1373), channel_id=1, replica_groups=mesh['groups'=2,'cells'=4,'corners'=2,'kern'=2] {'corners','kern'}, use_global_device_ids=true, to_apply=%region_11.14 | all-reduce | flops 8 | bytes 64 | tf_op jit(solution)/shard_map/psum | solution.py:142
  257.0 3.4 all-to-all-start.3
  260.5 9.1 %all-to-all-done.3 = bf16[4,8,32,128]{3,2,1,0:T(8,128)(2,1)S(1)} async-done(((bf16[4,8,32,128]{3,2,1,0:T(8,128)(2,1)}), bf16[4,8,32,128]{3,2,1,0:T(8,128)(2,1)S(1)}, u32[]{:S(2)}, u32[]{:S(2)}) %all-to-all-start.3) | async-done | bytes 262176 | tf_op jit(solution)/shard_map/all_to_all | solution.py:107
  271.7 3.0 gather_fusion.4
  276.3 5.6 %all_gather.7 = f32[2,128,128]{2,1,0:T(8,128)S(1)} all-gather(f32[2,32,128]{2,1,0:T(8,128)S(1)} %broadcast_multiply_fusion), channel_id=1, replica_groups=mesh['groups'=2,'cells'=4,'corners'=2,'kern'=2] {'corners','kern'}, dimensions={1}, use_global_device_ids=true | all-gather | bytes 163840 | tf_op jit(solution)/shard_map/all_gather | solution.py:119
  285.5 63.0 %while.94 = (s32[]{:T(128)}, f32[2,128,128]{1,2,0:T(8,128)S(1)}, f32[12,1,35,35]{3,2,1,0:T(8,128)S(1)}, f32[12,1,35,35]{3,2,1,0:T(8,128)S(1)}, f32[12,2,128,128]...) while((s32[]{:T(128)}, f32[2,128,128]{1,2,0:T(8,128)S(1)}, ...), condition=%wide.region_14.17_spmd.clone.clone.clone.clone, body=%wide.region_13.16_spmd.clone.clone.clone.clone.sunk | while | flops 70917336 | bytes 2136583 | solution.py:63
  349.3 16.2 %all-reduce.10.cloned.1.call-done = bf16[2,128,128]{1,2,0:T(8,128)(2,1)} async-done(((bf16[2,128,128]{1,2,0:T(8,128)(2,1)}), bf16[2,128,128]{1,2,0:T(8,128)(2,1)}) %all-reduce.10.cloned.1.call-update) | async-done | bytes 65552 | tf_op jit(solution)/shard_map/psum | solution.py:123
  366.4 56.9 %while.95 = (s32[]{:T(128)}, f32[2,35,35]{2,1,0:T(8,128)S(1)}, f32[2,35,35]{2,1,0:T(8,128)S(1)}, f32[12,1,35,35]{3,2,1,0:T(8,128)S(1)}, f32[12,2,128,128]{2,3,1,...) while((s32[]{:T(128)}, f32[2,35,35]{2,1,0:T(8,128)S(1)}, ...), condition=%wide.region_17.20_spmd.clone.clone.clone.clone, body=%wide.region_16.19_spmd.clone.clone.clone.clone.sunk | while | flops 70994280 | bytes 1536399 | solution.py:63
  426.3 32.9 %all-reduce.14.cloned.1.call-done = bf16[2,128,128]{2,0,1:T(2,128)(2,1)} async-done(((bf16[2,128,128]{2,0,1:T(2,128)(2,1)}), bf16[2,128,128]{2,0,1:T(2,128)(2,1)}) %all-reduce.14.cloned.1.call-update) | async-done | bytes 65552
  461.3 3.0 gather_fusion.5
  466.4 17.8 %all_to_all.27 = f32[4,8,32,128]{3,1,2,0:T(8,128)S(1)} all-to-all(f32[4,8,32,128]{3,1,2,0:T(8,128)S(1)} %fusion.354), channel_id=1, replica_groups=mesh['groups'=2,'cells'=4,'corners'=2,'kern'=2] {'cells'}, dimensions={0} | all-to-all | bytes 1048576 | tf_op jit(solution)/shard_map/all_to_all | solution.py:136
  484.6 5.7 %psum.31 = f32[8]{0:T(128)S(1)} all-reduce(f32[8]{0:T(128)S(1)} %get-tuple-element.1375), channel_id=1, replica_groups=mesh['groups'=2,'cells'=4,'corners'=2,'kern'=2] {'corners','kern'}, use_global_device_ids=true, to_apply=%region_20.23 | all-reduce | flops 8 | bytes 64 | tf_op jit(solution)/shard_map/psum | solution.py:142
  (608 shorter events, 280.1 us)
Async XLA Ops:
  6.5 11.9 %copy-start = (f32[8,128,128]{2,1,0:T(8,128)S(1)}, f32[8,128,128]{2,1,0:T(8,128)}, u32[]{:S(2)}) copy-start(f32[8,128,128]{2,1,0:T(8,128)} %param.19) | copy-start | bytes 1572868
  9.6 11.9 %all-to-all-start = ((s32[4,1,8]{2,1,0:T(1,128)}), s32[4,1,8]{2,1,0:T(1,128)S(1)}, u32[]{:S(2)}, u32[]{:S(2)}) async-start(s32[4,1,8]{2,1,0:T(1,128)} %bitcast.3), calls=%async_computation | async-start | bytes 4096 | tf_op jit(solution)/shard_map/all_to_all | solution.py:93
  18.4 8.8 %copy-start.3 = (f32[8,32,128]{2,1,0:T(8,128)}, f32[8,32,128]{2,1,0:T(8,128)S(1)}, u32[]{:S(2)}) copy-start(f32[8,32,128]{2,1,0:T(8,128)S(1)} %constant_dynamic-slice_fusion.2) | copy-start | bytes 393220
  23.7 10.5 %all-to-all-start.1 = ((bf16[4,8,32,128]{3,2,1,0:T(8,128)(2,1)}), bf16[4,8,32,128]{3,2,1,0:T(8,128)(2,1)S(1)}, u32[]{:S(2)}, u32[]{:S(2)}) async-start(bf16[4,8,32,128]{3,2,1,0:T(8,128)(2,1)} %copy.83), calls=%async_computation.1 | async-start | bytes 524288 | tf_op jit(solution)/shard_map/all_to_all | solution.py:107
  27.1 103.9 %all-reduce.8.cloned.1.call-start = ((), (), s32[]{:S(2)}) async-start(), calls=%async_computation.5 | async-start | bytes 131072 | tf_op jit(solution)/shard_map/psum | solution.py:123
  49.9 64.6 %copy-start.7 = (bf16[2,128,128]{2,1,0:T(8,128)(2,1)S(1)}, bf16[2,128,128]{2,1,0:T(8,128)(2,1)}, u32[]{:S(2)}) copy-start(bf16[2,128,128]{2,1,0:T(8,128)(2,1)} %param.20) | copy-start | bytes 196612
  113.6 111.2 %all-reduce.12.cloned.1.call-start = ((), (), s32[]{:S(2)}) async-start(), calls=%async_computation.7 | async-start | bytes 131072
  114.6 17.4 %copy-start.1 = (bf16[2,128,128]{1,2,0:T(8,128)(2,1)}, bf16[2,128,128]{1,2,0:T(8,128)(2,1)S(1)}, u32[]{:S(2)}) copy-start(bf16[2,128,128]{1,2,0:T(8,128)(2,1)S(1)} %copy.87) | copy-start | bytes 196612
  131.9 59.9 %copy-start.8 = (u32[32]{0:T(128)S(1)}, u32[32]{0:T(128)}, u32[]{:S(2)}) copy-start(u32[32]{0:T(128)} %constant.353) | copy-start | bytes 388
  229.8 19.9 %copy-start.4 = (f32[8,32,128]{2,1,0:T(8,128)S(1)}, f32[8,32,128]{2,1,0:T(8,128)}, u32[]{:S(2)}) copy-start(f32[8,32,128]{2,1,0:T(8,128)} %copy-done.3) | copy-start | bytes 393220
  256.0 14.3 %copy-start.5 = (f32[8,32,128]{2,0,1:T(8,128)}, f32[8,32,128]{2,0,1:T(8,128)S(1)}, u32[]{:S(2)}) copy-start(f32[8,32,128]{2,0,1:T(8,128)S(1)} %divide_subtract_fusion.1) | copy-start | bytes 393220
  257.0 12.6 %all-to-all-start.3 = ((bf16[4,8,32,128]{3,2,1,0:T(8,128)(2,1)}), bf16[4,8,32,128]{3,2,1,0:T(8,128)(2,1)S(1)}, u32[]{:S(2)}, u32[]{:S(2)}) async-start(bf16[4,8,32,128]{3,2,1,0:T(8,128)(2,1)} %copy.94), calls=%async_computation.3 | async-start | bytes 524288 | tf_op jit(solution)/shard_map/all_to_all | solution.py:107
  260.4 105.0 %all-reduce.10.cloned.1.call-start = ((), (), s32[]{:S(2)}) async-start(), calls=%async_computation.6 | async-start | bytes 131072 | tf_op jit(solution)/shard_map/psum | solution.py:123
  285.5 80.0 %copy-start.2 = (bf16[2,128,128]{1,2,0:T(8,128)(2,1)S(1)}, bf16[2,128,128]{1,2,0:T(8,128)(2,1)}, u32[]{:S(2)}) copy-start(bf16[2,128,128]{1,2,0:T(8,128)(2,1)} %copy-done.1) | copy-start | bytes 196612
  349.2 109.9 %all-reduce.14.cloned.1.call-start = ((), (), s32[]{:S(2)}) async-start(), calls=%async_computation.8 | async-start | bytes 131072
  464.3 19.9 %copy-start.6 = (f32[8,32,128]{2,0,1:T(8,128)S(1)}, f32[8,32,128]{2,0,1:T(8,128)}, u32[]{:S(2)}) copy-start(f32[8,32,128]{2,0,1:T(8,128)} %copy-done.5) | copy-start | bytes 393220
Sparse Core Ops, SparseCore 0:
  113.7 17.2 all-reduce.7
  192.0 32.7 all-reduce.11
  349.3 16.0 all-reduce.9
  426.4 32.7 all-reduce.13
where the time goes:
time: 502 us; the launch traced here: 498 us
  matrix products  211 us (42%)
  waiting for transfers between devices  116 us (23%)
  local copies, waits for them, and re-layouts  69.9 us (14%)
  blocking collectives  58 us (12%)
  between operations  15.1 us (3%)
  starting transfers between devices  13.5 us (3%)
  other arithmetic  11.2 us (2%)
    unnamed x6, waiting for transfers between devices  64.5 us
    dot_general x48, matrix products, add_kernel(): jnp.einsum('xf,tfy->txy', inv_imag, half_imag, precision=hp)  57.2 us
    dot_general x48, matrix products, add_kernel(): jnp.einsum('xf,tfy->txy', inv_real, half_real, precision=hp)  41.5 us
    all_to_all x2, blocking collectives, per_device(): lax.all_to_all(slot_grads, 'cells', split_axis=0, concat_axis=0, tiled=True)  35.6 us
    psum x2, waiting for transfers between devices, per_device(): lax.psum(partial_image.astype(jnp.bfloat16), 'kern').astype(jnp.float32)  32.6 us
    dot_general x48, matrix products, add_kernel(): jnp.einsum('xf,tfy->txy', inv_imag, half_real, precision=hp)  19.8 us
    dot_general x48, matrix products, add_kernel(): jnp.einsum('xf,tfy->txy', inv_real, half_imag, precision=hp)  19.5 us
    dynamic_update_slice x48, local copies, waits for them, and re-layouts, intensity(): result, unused = lax.scan(add_kernel, start, (kern_real, kern_imag))  18.1 us
  transfers between devices with their start and end apart: 7, of which 7 were waited for; matrix products, arithmetic and copies ran while one was open for 1% of the time, Pallas kernels for 0%

commit v1 on v0

--- a/solution.py
+++ b/solution.py
@@ -120,7 +120,9 @@
         partial_image, pullback = jax.vjp(
             lambda plane: intensity(plane, kern_real, kern_imag, tabs), tile_field
         )
-        image = lax.psum(partial_image.astype(jnp.bfloat16), "kern").astype(jnp.float32)
+        image = jnp.sum(
+            jax.lax.all_gather(partial_image.astype(jnp.bfloat16), "kern"), axis=0
+        ).astype(jnp.float32)
         resist = jax.nn.sigmoid(STEEP * (dose_now * image - 1.0))
         pressure = 2.0 * (resist - wanted) * resist * (1.0 - resist) * STEEP * dose_now
         tile_grad = pullback(pressure)[0]

time: 502 us -> 468 us (0.932)
  waiting for transfers between devices: 116 us -> 77.9 us
    psum x2 -> x0, waiting for transfers between devices: 32.6 us -> none  [per_device(): lax.psum(partial_image.astype(jnp.bfloat16), 'kern').astype(jnp.float32)]
    unnamed x6 -> x4, waiting for transfers between devices: 64.5 us -> 59.4 us
  transfers between devices with their start and end apart: 7 -> 5, of which waited for: 7 -> 5; matrix products, arithmetic and copies ran while one was open for 1% -> 1% of each run, Pallas kernels for 0% -> 0%
where the time goes in v1:
time: 468 us; the launch traced here: 463 us
  matrix products  211 us (45%)
  waiting for transfers between devices  77.9 us (17%)
  local copies, waits for them, and re-layouts  71.8 us (15%)
  blocking collectives  62 us (13%)
  between operations  15.3 us (3%)
  starting transfers between devices  13.2 us (3%)
  other arithmetic  8.44 us (2%)
    unnamed x4, waiting for transfers between devices  59.4 us
    dot_general x48, matrix products, add_kernel(): jnp.einsum('xf,tfy->txy', inv_imag, half_imag, precision=hp)  57.2 us
    dot_general x48, matrix products, add_kernel(): jnp.einsum('xf,tfy->txy', inv_real, half_real, precision=hp)  41.5 us
    all_to_all x2, blocking collectives, per_device(): lax.all_to_all(slot_grads, 'cells', split_axis=0, concat_axis=0, tiled=True)  35.6 us
    dot_general x48, matrix products, add_kernel(): jnp.einsum('xf,tfy->txy', inv_imag, half_real, precision=hp)  19.8 us
    dot_general x48, matrix products, add_kernel(): jnp.einsum('xf,tfy->txy', inv_real, half_imag, precision=hp)  19.5 us
    dynamic_update_slice x48, local copies, waits for them, and re-layouts, intensity(): result, unused = lax.scan(add_kernel, start, (kern_real, kern_imag))  18.6 us
    mul x48, local copies, waits for them, and re-layouts, add_kernel(): resp_real = pair[0] * spec_real - pair[1] * spec_imag  18.3 us
  transfers between devices with their start and end apart: 5, of which 5 were waited for; matrix products, arithmetic and copies ran while one was open for 1% of the time, Pallas kernels for 0%

profile of v1, /device:TPU:0, one launch (start us, length us, event | category | flops | bytes accessed | tf_op | source)
XLA Modules:
  0.0 463.1 jit_solution(18435872123845840357)
XLA Ops:
  9.6 6.3 %all-to-all-start = ((s32[4,1,8]{2,1,0:T(1,128)}), s32[4,1,8]{2,1,0:T(1,128)S(1)}, u32[]{:S(2)}, u32[]{:S(2)}) async-start(s32[4,1,8]{2,1,0:T(1,128)} %bitcast.3), calls=%async_computation | async-start | bytes 4096 | tf_op jit(solution)/shard_map/all_to_all | solution.py:93
  18.4 3.0 all-to-all-done
  23.7 3.4 all-to-all-start.1
  28.7 6.3 %all-to-all-done.1 = bf16[4,8,32,128]{3,2,1,0:T(8,128)(2,1)S(1)} async-done(((bf16[4,8,32,128]{3,2,1,0:T(8,128)(2,1)}), bf16[4,8,32,128]{3,2,1,0:T(8,128)(2,1)S(1)}, u32[]{:S(2)}, u32[]{:S(2)}) %all-to-all-start.1) | async-done | bytes 262176 | tf_op jit(solution)/shard_map/all_to_all | solution.py:107
  37.1 3.0 gather_fusion.1
  41.8 5.4 %all_gather.18 = f32[2,128,128]{2,1,0:T(8,128)S(1)} all-gather(f32[2,32,128]{2,1,0:T(8,128)S(1)} %broadcast_multiply_fusion.1), channel_id=1, replica_groups=mesh['groups'=2,'cells'=4,'corners'=2,'kern'=2] {'corners','kern'}, dimensions={1}, use_global_device_ids=true | all-gather | bytes 163840 | tf_op jit(solution)/shard_map/all_gather | solution.py:119
  50.7 63.5 %while.92 = (s32[]{:T(128)}, f32[2,128,128]{1,2,0:T(8,128)S(1)}, f32[12,1,35,35]{3,2,1,0:T(8,128)S(1)}, f32[12,1,35,35]{3,2,1,0:T(8,128)S(1)}, f32[12,2,128,128]...) while((s32[]{:T(128)}, f32[2,128,128]{1,2,0:T(8,128)S(1)}, ...), condition=%wide.region_5.8_spmd.clone.clone.clone.clone, body=%wide.region_4.7_spmd.clone.clone.clone.clone.sunk | while | flops 70917336 | bytes 2121003 | solution.py:63
  114.3 2.1 all-gather
  116.7 56.9 %while.93 = (s32[]{:T(128)}, f32[2,35,35]{2,1,0:T(8,128)S(1)}, f32[2,35,35]{2,1,0:T(8,128)S(1)}, f32[12,1,35,35]{3,2,1,0:T(8,128)S(1)}, f32[12,2,128,128]{2,3,1,...) while((s32[]{:T(128)}, f32[2,35,35]{2,1,0:T(8,128)S(1)}, ...), condition=%wide.region_8.11_spmd.clone.clone.clone.clone, body=%wide.region_7.10_spmd.clone.clone.clone.clone.sunk | while | flops 70994280 | bytes 1536399 | solution.py:63
  177.8 29.3 %all-reduce.6.cloned.1.call-done = bf16[2,128,128]{2,0,1:T(2,128)(2,1)} async-done(((bf16[2,128,128]{2,0,1:T(2,128)(2,1)}), bf16[2,128,128]{2,0,1:T(2,128)(2,1)}) %all-reduce.6.cloned.1.call-update) | async-done | bytes 65552
  209.3 3.0 gather_fusion.2
  214.4 17.8 %all_to_all.26 = f32[4,8,32,128]{3,1,2,0:T(8,128)S(1)} all-to-all(f32[4,8,32,128]{3,1,2,0:T(8,128)S(1)} %fusion.356), channel_id=1, replica_groups=mesh['groups'=2,'cells'=4,'corners'=2,'kern'=2] {'cells'}, dimensions={0} | all-to-all | bytes 1048576 | tf_op jit(solution)/shard_map/all_to_all | solution.py:138
  232.6 5.7 %psum.14 = f32[8]{0:T(128)S(1)} all-reduce(f32[8]{0:T(128)S(1)} %get-tuple-element.1427), channel_id=1, replica_groups=mesh['groups'=2,'cells'=4,'corners'=2,'kern'=2] {'corners','kern'}, use_global_device_ids=true, to_apply=%region_11.14 | all-reduce | flops 8 | bytes 64 | tf_op jit(solution)/shard_map/psum | solution.py:144
  240.1 3.4 all-to-all-start.3
  243.6 9.1 %all-to-all-done.3 = bf16[4,8,32,128]{3,2,1,0:T(8,128)(2,1)S(1)} async-done(((bf16[4,8,32,128]{3,2,1,0:T(8,128)(2,1)}), bf16[4,8,32,128]{3,2,1,0:T(8,128)(2,1)S(1)}, u32[]{:S(2)}, u32[]{:S(2)}) %all-to-all-start.3) | async-done | bytes 262176 | tf_op jit(solution)/shard_map/all_to_all | solution.py:107
  254.7 3.0 gather_fusion.4
  259.4 5.6 %all_gather.21 = f32[2,128,128]{2,1,0:T(8,128)S(1)} all-gather(f32[2,32,128]{2,1,0:T(8,128)S(1)} %broadcast_multiply_fusion), channel_id=1, replica_groups=mesh['groups'=2,'cells'=4,'corners'=2,'kern'=2] {'corners','kern'}, dimensions={1}, use_global_device_ids=true | all-gather | bytes 163840 | tf_op jit(solution)/shard_map/all_gather | solution.py:119
  268.6 63.5 %while.94 = (s32[]{:T(128)}, f32[2,128,128]{1,2,0:T(8,128)S(1)}, f32[12,1,35,35]{3,2,1,0:T(8,128)S(1)}, f32[12,1,35,35]{3,2,1,0:T(8,128)S(1)}, f32[12,2,128,128]...) while((s32[]{:T(128)}, f32[2,128,128]{1,2,0:T(8,128)S(1)}, ...), condition=%wide.region_14.17_spmd.clone.clone.clone.clone, body=%wide.region_13.16_spmd.clone.clone.clone.clone.sunk | while | flops 70917336 | bytes 2121003 | solution.py:63
  332.2 1.9 all-gather.1
  334.3 56.9 %while.95 = (s32[]{:T(128)}, f32[2,35,35]{2,1,0:T(8,128)S(1)}, f32[2,35,35]{2,1,0:T(8,128)S(1)}, f32[12,1,35,35]{3,2,1,0:T(8,128)S(1)}, f32[12,2,128,128]{2,3,1,...) while((s32[]{:T(128)}, f32[2,35,35]{2,1,0:T(8,128)S(1)}, ...), condition=%wide.region_17.20_spmd.clone.clone.clone.clone, body=%wide.region_16.19_spmd.clone.clone.clone.clone.sunk | while | flops 70994280 | bytes 1536399 | solution.py:63
  394.2 30.1 %all-reduce.8.cloned.1.call-done = bf16[2,128,128]{2,0,1:T(2,128)(2,1)} async-done(((bf16[2,128,128]{2,0,1:T(2,128)(2,1)}), bf16[2,128,128]{2,0,1:T(2,128)(2,1)}) %all-reduce.8.cloned.1.call-update) | async-done | bytes 65552
  426.4 3.0 gather_fusion.5
  431.5 17.8 %all_to_all.27 = f32[4,8,32,128]{3,1,2,0:T(8,128)S(1)} all-to-all(f32[4,8,32,128]{3,1,2,0:T(8,128)S(1)} %fusion.354), channel_id=1, replica_groups=mesh['groups'=2,'cells'=4,'corners'=2,'kern'=2] {'cells'}, dimensions={0} | all-to-all | bytes 1048576 | tf_op jit(solution)/shard_map/all_to_all | solution.py:138
  449.8 5.7 %psum.15 = f32[8]{0:T(128)S(1)} all-reduce(f32[8]{0:T(128)S(1)} %get-tuple-element.1429), channel_id=1, replica_groups=mesh['groups'=2,'cells'=4,'corners'=2,'kern'=2] {'corners','kern'}, use_global_device_ids=true, to_apply=%region_20.23 | all-reduce | flops 8 | bytes 64 | tf_op jit(solution)/shard_map/psum | solution.py:144
  (601 shorter events, 278.9 us)
Async XLA Ops:
  6.5 11.9 %copy-start = (f32[8,128,128]{2,1,0:T(8,128)S(1)}, f32[8,128,128]{2,1,0:T(8,128)}, u32[]{:S(2)}) copy-start(f32[8,128,128]{2,1,0:T(8,128)} %param.19) | copy-start | bytes 1572868
  9.6 11.8 %all-to-all-start = ((s32[4,1,8]{2,1,0:T(1,128)}), s32[4,1,8]{2,1,0:T(1,128)S(1)}, u32[]{:S(2)}, u32[]{:S(2)}) async-start(s32[4,1,8]{2,1,0:T(1,128)} %bitcast.3), calls=%async_computation | async-start | bytes 4096 | tf_op jit(solution)/shard_map/all_to_all | solution.py:93
  23.7 11.3 %all-to-all-start.1 = ((bf16[4,8,32,128]{3,2,1,0:T(8,128)(2,1)}), bf16[4,8,32,128]{3,2,1,0:T(8,128)(2,1)S(1)}, u32[]{:S(2)}, u32[]{:S(2)}) async-start(bf16[4,8,32,128]{3,2,1,0:T(8,128)(2,1)} %copy.115), calls=%async_computation.1 | async-start | bytes 524288 | tf_op jit(solution)/shard_map/all_to_all | solution.py:107
  27.2 180.0 %all-reduce.6.cloned.1.call-start = ((), (), s32[]{:S(2)}) async-start(), calls=%async_computation.5 | async-start | bytes 131072
  50.7 65.7 %copy-start.3 = (bf16[2,128,128]{2,1,0:T(8,128)(2,1)S(1)}, bf16[2,128,128]{2,1,0:T(8,128)(2,1)}, u32[]{:S(2)}) copy-start(bf16[2,128,128]{2,1,0:T(8,128)(2,1)} %param.20) | copy-start | bytes 196612
  116.7 59.9 %copy-start.5 = (u32[32]{0:T(128)S(1)}, u32[32]{0:T(128)}, u32[]{:S(2)}) copy-start(u32[32]{0:T(128)} %constant.356) | copy-start | bytes 388
  238.4 0.7 copy-start.1
  240.1 12.6 %all-to-all-start.3 = ((bf16[4,8,32,128]{3,2,1,0:T(8,128)(2,1)}), bf16[4,8,32,128]{3,2,1,0:T(8,128)(2,1)S(1)}, u32[]{:S(2)}, u32[]{:S(2)}) async-start(bf16[4,8,32,128]{3,2,1,0:T(8,128)(2,1)} %copy.127), calls=%async_computation.3 | async-start | bytes 524288 | tf_op jit(solution)/shard_map/all_to_all | solution.py:107
  243.5 180.8 %all-reduce.8.cloned.1.call-start = ((), (), s32[]{:S(2)}) async-start(), calls=%async_computation.6 | async-start | bytes 131072
  268.6 65.5 %copy-start.4 = (bf16[2,128,128]{2,1,0:T(8,128)(2,1)S(1)}, bf16[2,128,128]{2,1,0:T(8,128)(2,1)}, u32[]{:S(2)}) copy-start(bf16[2,128,128]{2,1,0:T(8,128)(2,1)} %param.20) | copy-start | bytes 196612
  429.4 19.9 %copy-start.2 = (f32[8,32,128]{2,0,1:T(8,128)S(1)}, f32[8,32,128]{2,0,1:T(8,128)}, u32[]{:S(2)}) copy-start(f32[8,32,128]{2,0,1:T(8,128)} %copy-done.1) | copy-start | bytes 393220
Sparse Core Ops, SparseCore 0:
  176.7 30.4 all-reduce.5
  394.3 29.8 all-reduce.7
